TPU v7x, 768 devices: a whole 4x8x12 slice. The times are simulated.
768 devices in a mesh: dp: 128 (over y, x, z_hi), ctx: 6 (over z_lo, core).
Axes of the slice: x: 4, y: 8, z: 12 (z_hi: 4, z_lo: 3; z = z_hi * 3 + z_lo), core: 2. Of those that a mesh axis runs over, the one named last changes fastest.
Arguments:
- queries: bfloat16 [128, 768, 128], P('dp', 'ctx'), may hold values from -6 to 6
- key_vectors: bfloat16 [128, 768, 128], P('dp', 'ctx'), may hold values from -6 to 6
- value_vectors: bfloat16 [128, 768, 128], P('dp', 'ctx'), may hold values from -6 to 6
- log_decay: float32 [128, 768, 128], P('dp', 'ctx'), may hold values from -2 to 0, as said below
- out_weight: bfloat16 [5120, 128], replicated, may hold values from -0.5 to 0.5
- cotangent: bfloat16 [128, 768, 5120], P('dp', 'ctx'), may hold values from -1.25 to 1.25
Outputs:
- grad_queries: bfloat16 [128, 768, 128], P('dp', 'ctx')
- grad_keys: bfloat16 [128, 768, 128], P('dp', 'ctx')
- grad_values: bfloat16 [128, 768, 128], P('dp', 'ctx')
- grad_decay: float32 [128, 768, 128], P('dp', 'ctx')
- grad_weight: float32 [5120, 128], P('dp')
Inputs may be any that keep to these rules, and one draw needn't show every extreme that they name: `log_decay`: every entry is negative.
All inputs are finite; a program needn't handle non-finite values.
Results may differ from a plain program's by a relative error of at most 0.0029.
Values sent between devices are 32-bit elements; how exact they have to be, the bound alone decides.
A program may use at most 32 MiB of HBM per device.

v0:
```python
import jax
import jax.numpy as jnp
from jax import lax
from jax.sharding import PartitionSpec as P

DK = 128
HEADS = 1
BLK = 128


EPSILON = 1e-05
PRECISE = lax.Precision.HIGHEST


def shifted(value, axis, steps):
    count = lax.axis_size(axis)
    leading, last = (max(0, -steps), min(count, count - steps))
    return lax.ppermute(value, axis, [(source, source + steps) for source in range(leading, last)])


def body(queries, key_vectors, value_vectors, log_decay, out_weight, cotangent):
    length = queries.shape[1]
    blocks = length // BLK
    shaped = (blocks, BLK, HEADS, DK)
    query_blk = queries.reshape(shaped).astype(jnp.float32)
    key_blk = key_vectors.reshape(shaped).astype(jnp.float32)
    value_blk = value_vectors.reshape(shaped).astype(jnp.float32)
    decay_blk = log_decay.reshape(shaped)
    lower = jnp.tril(jnp.ones((BLK, BLK), jnp.float32))
    cumul = jnp.einsum("ij,njhc->nihc", lower, decay_blk, precision=PRECISE)
    totals = cumul[:, -1]
    rising = jnp.exp(cumul)
    falling = jnp.exp(-cumul)
    to_end = jnp.exp(totals[:, None] - cumul)
    query_scaled = query_blk * rising
    key_scaled = key_blk * falling
    key_to_end = key_blk * to_end
    scores = jnp.einsum("nihc,njhc->nhij", query_scaled, key_scaled, precision=PRECISE) * lower
    within = jnp.einsum("nhij,njhe->nihe", scores, value_blk, precision=PRECISE)
    block_states = jnp.einsum("njhc,njhe->nhce", key_to_end, value_blk, precision=PRECISE)

    def advance(carry, inputs):
        block_decay, block_state = inputs
        return (jnp.exp(block_decay)[..., None] * carry + block_state, carry)

    zero_state = jnp.zeros((HEADS, DK, DK), jnp.float32)
    local_state, zero_entries = lax.scan(advance, zero_state, (totals, block_states))
    before = jnp.cumsum(totals, axis=0) - totals
    device_decay = jnp.sum(totals, axis=0)
    after = device_decay - before - totals
    steps_count = lax.axis_size("ctx") - 1

    def pass_state(turn_index, incoming):
        return shifted(local_state + jnp.exp(device_decay)[..., None] * incoming, "ctx", 1)

    state_in = lax.fori_loop(0, steps_count, pass_state, zero_state)
    entries = zero_entries + jnp.exp(before)[..., None] * state_in
    across = jnp.einsum("nihc,nhce->nihe", query_scaled, entries, precision=PRECISE)
    output = within + across
    scale_inv = lax.rsqrt(jnp.mean(output * output, axis=-1, keepdims=True) + EPSILON)
    normed = output * scale_inv
    rounded = normed.reshape(length, HEADS * DK).astype(jnp.bfloat16)
    upstream = cotangent.reshape(length, cotangent.shape[2])
    row_share = lax.psum_scatter(
        jnp.einsum("td,tk->dk", upstream, rounded, preferred_element_type=jnp.float32),
        "dp",
        scatter_dimension=0,
        tiled=True,
    )
    grad_weight = lax.psum(row_share, "ctx")
    grad_normed = jnp.dot(upstream, out_weight, preferred_element_type=jnp.float32).reshape(shaped)
    grad_output = scale_inv * (
        grad_normed - normed * jnp.mean(grad_normed * normed, axis=-1, keepdims=True)
    )
    pairs = jnp.einsum("nihe,njhe->nhij", grad_output, value_blk, precision=PRECISE) * lower
    grad_query = rising * (
        jnp.einsum("nhij,njhc->nihc", pairs, key_scaled, precision=PRECISE)
        + jnp.einsum("nihe,nhce->nihc", grad_output, entries, precision=PRECISE)
    )
    block_grads = jnp.einsum("nihc,nihe->nhce", query_scaled, grad_output, precision=PRECISE)

    def retreat(carry, inputs):
        block_decay, block_grad = inputs
        return (block_grad + jnp.exp(block_decay)[..., None] * carry, carry)

    local_grad, zero_after = lax.scan(retreat, zero_state, (totals, block_grads), reverse=True)
    grad_key_zero = falling * jnp.einsum(
        "nhij,nihc->njhc", pairs, query_scaled, precision=PRECISE
    ) + to_end * jnp.einsum("nhce,njhe->njhc", zero_after, value_blk, precision=PRECISE)
    grad_value_zero = jnp.einsum(
        "nhij,nihe->njhe", scores, grad_output, precision=PRECISE
    ) + jnp.einsum("njhc,nhce->njhe", key_to_end, zero_after, precision=PRECISE)
    gate_zero = query_blk * grad_query - key_blk * grad_key_zero
    sigma_zero = jnp.sum(gate_zero, axis=(0, 1))

    def pass_grad(turn_index, carried):
        grad_in, later_sum = carried
        own_sum = sigma_zero - jnp.sum(grad_in * local_state, axis=-1)
        return shifted(
            (local_grad + jnp.exp(device_decay)[..., None] * grad_in, own_sum + later_sum),
            "ctx",
            -1,
        )

    grad_in, later_sum = lax.fori_loop(
        0, steps_count, pass_grad, (zero_state, jnp.zeros_like(sigma_zero))
    )
    reach = to_end * jnp.exp(after)[:, None]
    grad_key = grad_key_zero + reach * jnp.einsum(
        "hce,njhe->njhc", grad_in, value_blk, precision=PRECISE
    )
    grad_value = grad_value_zero + jnp.einsum(
        "njhc,hce->njhe", key_blk * reach, grad_in, precision=PRECISE
    )
    gate_full = query_blk * grad_query - key_blk * grad_key
    within_suffix = jnp.einsum("ij,njhc->nihc", jnp.transpose(lower), gate_full, precision=PRECISE)
    block_totals = jnp.sum(gate_full, axis=1)
    later_blocks = jnp.sum(block_totals, axis=0) - jnp.cumsum(block_totals, axis=0)
    grad_gate = within_suffix + later_blocks[:, None] + later_sum
    flat = (1, length, HEADS * DK)
    return (
        grad_query.reshape(flat).astype(jnp.bfloat16),
        grad_key.reshape(flat).astype(jnp.bfloat16),
        grad_value.reshape(flat).astype(jnp.bfloat16),
        grad_gate.reshape(flat),
        grad_weight,
    )


def solution(mesh):
    placed = (
        P("dp", "ctx", None),
        P("dp", "ctx", None),
        P("dp", "ctx", None),
        P("dp", "ctx", None),
        P(),
        P("dp", "ctx", None),
    )
    return jax.shard_map(
        body,
        mesh=mesh,
        in_specs=placed,
        out_specs=(
            P("dp", "ctx", None),
            P("dp", "ctx", None),
            P("dp", "ctx", None),
            P("dp", "ctx", None),
            P("dp", None),
        ),
        check_vma=False,
    )
```

profile of v0, /device:TPU:1, one launch (start us, length us, event | category | flops | bytes accessed | tf_op | source)
XLA Modules:
  0.0 1631.3 jit_solution(9200723682545964084)
XLA Ops:
  7.2 1.1 convolution_bitcast_fusion.8
  8.4 1.1 convolution_multiply_fusion.1
  9.5 1.0 convolution_bitcast_fusion.7
  10.5 1.0 fusion.9
  11.5 33.0 %while.8 = (s32[]{:T(128)}, f32[1,128,128]{2,1,0:T(8,128)S(1)}, f32[1,128,1]{1,2,0:T(1,128)S(1)}, f32[1,128,128]{2,1,0:T(8,128)S(1)}, s32[]{:T(128)}) while((s32[]{:T(128)}, f32[1,128,128]{2,1,0:T(8,128)S(1)}, f32[1,128,1]{1,2,0:T(1,128)S(1)}, f32[1,128,128]{2,1,0:T(8,128)S(1)}, s32[]{:T(128)}) %tuple.66), condition=%wide.region_1.2_spmd, body=%wide.region_0.1_spmd.sunk | while | flops 32770 | bytes 459365 | solution.py:56
  11.5 0.1 multiply_add_fusion.3
  11.6 5.4 collective-permute-start
  17.0 7.1 collective-permute-done
  24.1 0.1 multiply_add_fusion.3
  24.2 1.9 collective-permute-start
  26.1 1.3 collective-permute-done
  27.5 0.1 multiply_add_fusion.3
  27.5 4.3 collective-permute-start
  31.8 1.3 collective-permute-done
  33.2 4.3 collective-permute-start
  37.5 1.3 collective-permute-done
  38.8 0.1 multiply_add_fusion.3
  38.9 4.3 collective-permute-start
  43.2 1.3 collective-permute-done
  44.5 0.4 multiply_reduce_fusion.2
  44.9 2.0 convolution_bitcast_fusion
  46.9 0.7 copy-done.4
  47.7 0.2 fusion.13
  47.8 0.4 copy-done.2
  48.2 0.7 fusion.42
  48.9 0.2 convolution_multiply_fusion
  49.2 0.3 fusion.4
  49.5 0.1 multiply_reduce_fusion.1
  49.6 0.2 fusion.50
  49.9 0.3 fusion.22
  50.2 0.3 fusion.31
  50.5 35.8 %while.18 = (s32[]{:T(128)}, f32[1,128,128]{2,1,0:T(8,128)S(1)}, f32[1,128]{1,0:T(1,128)S(1)}, f32[1,128,1]{1,2,0:T(1,128)S(1)}, f32[1,128,128]{2,1,0:T(8,128)S(...) while((s32[]{:T(128)}, f32[1,128,128]{2,1,0:T(8,128)S(1)}, f32[1,128]{1,0:T(1,128)S(1)}, ...), condition=%wide.region_7.8_spmd, body=%wide.region_5.7_spmd.sunk | while | flops 65666 | bytes 529573 | solution.py:105
  50.5 0.1 multiply_reduce_fusion.4
  50.6 1.9 collective-permute-start.1
  52.6 1.9 collective-permute-start.2
  54.5 3.6 collective-permute-done.2
  58.1 0.1 multiply_reduce_fusion.4
  58.2 1.9 collective-permute-start.1
  60.2 1.9 collective-permute-start.2
  62.1 3.0 collective-permute-done.2
  65.0 0.1 multiply_reduce_fusion.4
  65.2 1.9 collective-permute-start.1
  67.1 1.9 collective-permute-start.2
  69.0 3.0 collective-permute-done.2
  72.0 0.1 multiply_reduce_fusion.4
  72.1 1.9 collective-permute-start.1
  74.1 1.9 collective-permute-start.2
  76.0 3.0 collective-permute-done.2
  78.9 0.1 multiply_reduce_fusion.4
  79.1 1.9 collective-permute-start.1
  81.0 1.9 collective-permute-start.2
  82.9 3.4 collective-permute-done.2
  86.3 0.3 convolution_bitcast_fusion.2
  86.6 0.2 fusion.24
  86.8 0.7 copy.14
  87.5 0.2 fusion.15
  87.8 0.7 fusion.86
  88.4 0.3 fusion.21
  88.7 0.7 copy.15
  89.4 1.3 dynamic-slice
  91.4 1432.0 %all-reduce.3.cloned.1.call-done = f32[5120,128]{0,1:T(8,128)} async-done(((f32[5120,128]{0,1:T(8,128)}), f32[5120,128]{0,1:T(8,128)}) %all-reduce.3.cloned.1.call-update) | async-done | bytes 2621456
  1523.3 1.0 constant_dynamic-slice_fusion
  1524.3 99.5 %psum.7 = f32[40,128]{0,1:T(8,128)S(1)} all-reduce(f32[40,128]{0,1:T(8,128)S(1)} %constant_dynamic-slice_fusion), channel_id=1, replica_groups=mesh['dp'=128,'ctx'=6] {'ctx'}, use_global_device_ids=true, to_apply=%region_11.12 | all-reduce | flops 5120 | bytes 40960 | tf_op jit(solution)/shard_map/psum | solution.py:70
  1623.8 0.7 copy.16
  (30 shorter events, 0.3 us)
Async XLA Ops:
  7.2 37.7 %copy-start = (bf16[1,128,5120]{2,1,0:T(8,128)(2,1)S(1)}, bf16[1,128,5120]{2,1,0:T(8,128)(2,1)}, u32[]{:S(2)}) copy-start(bf16[1,128,5120]{2,1,0:T(8,128)(2,1)} %param.15) | copy-start | bytes 3932164
  7.2 37.3 %copy-start.3 = (bf16[1,128,128]{2,1,0:T(8,128)(2,1)S(1)}, bf16[1,128,128]{2,1,0:T(8,128)(2,1)}, u32[]{:S(2)}) copy-start(bf16[1,128,128]{2,1,0:T(8,128)(2,1)} %param.10) | copy-start | bytes 98308
  7.2 1516.1 %all-reduce.3.cloned.1.call-start = ((), (), s32[]{:S(2)}) async-start(), calls=%async_computation | async-start | bytes 5242880
  11.6 12.5 collective-permute-start
  24.2 3.2 collective-permute-start
  27.5 5.6 collective-permute-start
  33.2 5.6 collective-permute-start
  38.9 5.6 collective-permute-start
  46.9 0.8 copy-start.4
  46.9 1.3 copy-start.2
  48.2 1.3 copy-start.1
  50.6 7.5 collective-permute-start.1
  52.6 5.5 collective-permute-start.2
  58.2 6.8 collective-permute-start.1
  60.2 4.9 collective-permute-start.2
  65.2 6.8 collective-permute-start.1
  67.1 4.9 collective-permute-start.2
  72.1 6.8 collective-permute-start.1
  74.1 4.9 collective-permute-start.2
  79.1 7.2 collective-permute-start.1
  81.0 5.3 collective-permute-start.2
Sparse Core Ops, SparseCore 0:
  47.1 1476.2 all-reduce.2
where the time goes:
time: 1630 us
  waiting for transfers between devices  1460 us (90%)
  blocking collectives  99.5 us (6%)
  starting transfers between devices  39.3 us (2%)
    unnamed x2, waiting for transfers between devices  1430 us
    psum x1, blocking collectives, body(): grad_weight = lax.psum(row_share, 'ctx')  99.5 us
    ppermute x15, starting transfers between devices, shifted(): lax.ppermute(value, axis, [(source, source + steps) for source in range(l...  39.3 us
  transfers between devices with their start and end apart: 16, of which 11 were waited for; matrix products, arithmetic and copies ran while one was open for 0% of the time, Pallas kernels for 0%

commit v1 on v0

v1 whole, which is shorter than its diff:
```python
import jax
import jax.numpy as jnp
from jax import lax
from jax.experimental import pallas as pl
from jax.experimental.pallas import tpu as pltpu
from jax.sharding import PartitionSpec as P

X, Y, Z, ZL, ZH = 4, 8, 12, 3, 4
T = 128
C = 128
D = 5120
R = D // (X * Y * ZH)
EPSILON = 1e-05
MESH = pl.DeviceIdType.MESH
F32 = jnp.float32
BF16 = jnp.bfloat16


def mm(a, b, dims=((1,), (0,)), precision=lax.Precision.HIGHEST):
    return lax.dot_general(a, b, (dims, ((), ())), precision=precision, preferred_element_type=F32)


NT = ((1,), (1,))
TN = ((0,), (0,))


class Ring:
    def __init__(self, me, count, device, own, streams, slots, send, recv):
        self.me, self.count, self.device, self.own = me, count, device, own
        self.slots, self.send, self.recv = slots, send, recv
        self.streams, base = [], 0
        for part, sign, hops in streams:
            self.streams.append((part, sign, hops, base))
            base += hops

    def dest(self, stream, turn):
        _, sign, hops, _ = self.streams[stream]
        return lax.rem(self.me + sign * (hops - turn) + self.count, self.count)

    def copy(self, stream, turn):
        part, sign, _, base = self.streams[stream]
        source = self.own(self.dest(stream, 0), part) if turn == 0 else self.slots.at[base + turn - 1]
        return pltpu.make_async_remote_copy(
            src_ref=source,
            dst_ref=self.slots.at[base + turn],
            send_sem=self.send.at[base + turn],
            recv_sem=self.recv.at[base + turn],
            device_id=self.device(sign),
            device_id_type=MESH,
        )

    def start(self, stream):
        self.copy(stream, 0).start()

    def step(self, stream, turn):
        part, _, _, base = self.streams[stream]
        self.copy(stream, turn - 1).wait_recv()
        self.slots[base + turn - 1] += self.own(self.dest(stream, turn), part)[...]
        self.copy(stream, turn).start()

    def finish(self, stream):
        part, _, hops, base = self.streams[stream]
        self.copy(stream, hops - 1).wait_recv()
        self.own(self.me, part)[...] += self.slots[base + hops - 1]

    def drain(self):
        for index, (_, _, hops, _) in enumerate(self.streams):
            for turn in range(hops):
                self.copy(index, turn).wait_send()


def kernel(
    q_hbm, k_hbm, v_hbm, decay_hbm, weight_hbm, cot_hbm,
    gq_ref, gk_ref, gv_ref, gd_ref, gw_ref,
    q_in, k_in, v_in, decay_in, weight_in, cot_in, cot_t, in_sem,
    acc, pair_slots, pair_send, pair_recv,
    x1_slots, x1_send, x1_recv, y1_slots, y1_send, y1_recv,
    x2_slots, x2_send, x2_recv, y2_slots, y2_send, y2_recv,
    z_slots, z_send, z_recv, w_out, w_send, w_recv,
    f_loc, f_mate, f_pair, f_in, f_mate_send, f_mate_recv, f_send, f_recv,
    b_loc, b_mate, b_pair, b_in, b_mate_send, b_mate_recv, b_send, b_recv,
):
    dp, ctx = lax.axis_index("dp"), lax.axis_index("ctx")
    yy = dp // (X * ZH)
    xx = (dp // ZH) % X
    zz = (dp % ZH) * ZL + ctx // 2
    core = ctx % 2
    chip = ctx // 2

    def at(y, x, z, h):
        return {"dp": (y * X + x) * ZH + z // ZL, "ctx": (z % ZL) * 2 + h}

    def near_x(sign):
        return at(yy, lax.rem(xx + sign + X, X), zz, core)

    def near_y(sign):
        return at(lax.rem(yy + sign + Y, Y), xx, zz, core)

    mate = at(yy, xx, zz, 1 - core)
    base_z = 6 * core
    gathers = zz // 6 == core

    operands = (
        (decay_hbm, decay_in), (k_hbm, k_in), (v_hbm, v_in), (q_hbm, q_in), (cot_hbm, cot_in), (weight_hbm, weight_in),
    )
    loads = [pltpu.make_async_copy(a, b, in_sem.at[i]) for i, (a, b) in enumerate(operands)]
    for load in loads:
        load.start()

    barrier = pltpu.get_barrier_semaphore()

    def greet(device):
        pl.semaphore_signal(barrier, inc=1, device_id=device, device_id_type=MESH)

    @pl.when(gathers)
    def _():
        for far in (6, 5, 7, 4, 8, 3, 9, 2, 10, 1, 11):
            greet(at(yy, xx, lax.rem(zz + far, Z), core))

    @pl.when(jnp.logical_not(gathers))
    def _():
        for i in range(6):
            greet(at(yy, xx, base_z + i, core))

    for sign in (1, -1):
        greet(near_y(sign))
        greet(near_x(sign))
    for step in range(1, 6):
        greet({"dp": dp, "ctx": lax.rem(ctx + step, 6)})

    row = lax.broadcasted_iota(jnp.int32, (T, T), 0)
    column = lax.broadcasted_iota(jnp.int32, (T, T), 1)
    lower = (row >= column).astype(F32)
    loads[0].wait()
    cumul = mm(lower, decay_in[...])
    total = cumul[T - 1 : T, :]
    decay = jnp.exp(total)
    loads[1].wait()
    loads[2].wait()
    key = k_in[...].astype(F32)
    value = v_in[...].astype(F32)
    key_to_end = key * jnp.exp(total - cumul)
    local = mm(value, key_to_end, TN)
    f_loc[:C, :] = local
    f_loc[C:, :] = jnp.broadcast_to(decay, (8, C))

    @pl.when(gathers)
    def _():
        pl.semaphore_wait(barrier, 20)

    @pl.when(jnp.logical_not(gathers))
    def _():
        pl.semaphore_wait(barrier, 15)

    def far_sends(pair, slots, send, recv, first, last):
        def copy(slot, target, h, index):
            return pltpu.make_async_remote_copy(
                pair, slots.at[slot], send.at[index], recv.at[slot],
                device_id={"dp": dp, "ctx": 2 * target + h}, device_id_type=MESH,
            )

        from_first = [copy(0, last, h, h) for h in (0, 1)] + [copy(0, 1, h, 2 + h) for h in (0, 1)]
        from_middle = [copy(1, last, h, h) for h in (0, 1)]
        return from_first, from_middle

    f_first, f_middle = far_sends(f_pair, f_in, f_send, f_recv, 0, 2)
    b_first, b_middle = far_sends(b_pair, b_in, b_send, b_recv, 2, 0)
    f_to_mate = pltpu.make_async_remote_copy(
        f_loc, f_mate, f_mate_send, f_mate_recv, device_id=mate, device_id_type=MESH
    )
    b_to_mate = pltpu.make_async_remote_copy(
        b_loc, b_mate, b_mate_send, b_mate_recv, device_id=mate, device_id_type=MESH
    )
    even = core == 0
    odd = core == 1

    @pl.when(even)
    def _():
        f_to_mate.start()

    loads[3].wait()
    query = q_in[...].astype(F32)
    rising = jnp.exp(cumul)
    falling = jnp.exp(-cumul)
    query_scaled = query * rising
    key_scaled = key * falling
    scores = mm(query_scaled, key_scaled, NT) * lower

    @pl.when(odd)
    def _():
        f_to_mate.wait_recv()
        f_pair[:C, :] = f_loc[C : C + 1, :] * f_mate[:C, :] + f_loc[:C, :]
        f_pair[C:, :] = f_loc[C:, :] * f_mate[C:, :]

        @pl.when(chip == 0)
        def _():
            for copy in f_first:
                copy.start()

        @pl.when(chip == 1)
        def _():
            for copy in f_middle:
                copy.start()

    within = mm(scores, value)
    loads[4].wait()
    for i in range(D // 128):
        cot_t[128 * i : 128 * (i + 1), :] = cot_in[:, 128 * i : 128 * (i + 1)].T
    loads[5].wait()
    grad_normed = jnp.dot(cot_in[...], weight_in[...], preferred_element_type=F32)

    def carried(slots, copies_first, copies_middle, here_first, here_last, loc_in):
        @pl.when(chip == here_first)
        def _():
            loc_in[...] = jnp.zeros_like(loc_in)

        @pl.when(chip == 1)
        def _():
            copies_first[0].wait_recv()
            loc_in[...] = slots[0, :C, :]

        @pl.when(chip == here_last)
        def _():
            copies_first[0].wait_recv()
            copies_middle[0].wait_recv()
            loc_in[...] = slots[1, C : C + 1, :] * slots[0, :C, :] + slots[1, :C, :]

    state_ref = w_out.at[0:C]
    carried(f_in, f_first, f_middle, 0, 2, state_ref)

    @pl.when(odd)
    def _():
        state_ref[...] = f_mate[C : C + 1, :] * state_ref[...] + f_mate[:C, :]

    state_in = state_ref[...]
    output = within + mm(query_scaled, state_in, NT)
    scale_inv = lax.rsqrt(jnp.mean(output * output, axis=-1, keepdims=True) + EPSILON)
    normed = output * scale_inv
    rounded = normed.astype(BF16)

    mine, theirs = 2 * core, 2 * (1 - core)
    x_order = (2, 1, 3, 0)
    y_order = (4, 3, 5, 2, 6, 1, 7, 0)

    def x_pair(k):
        there = lax.rem(xx + x_order[k], X)
        return there, pltpu.make_async_remote_copy(
            acc.at[:, there, theirs],
            pair_slots.at[0, :, there],
            pair_send.at[k],
            pair_recv.at[k],
            device_id=mate,
            device_id_type=MESH,
        )

    def y_pair(k):
        there = lax.rem(yy + y_order[k], Y)
        return there, pltpu.make_async_remote_copy(
            acc.at[there, :, theirs + 1],
            pair_slots.at[1, there],
            pair_send.at[X + k],
            pair_recv.at[X + k],
            device_id=mate,
            device_id_type=MESH,
        )

    for k in range(X):
        there, copy = x_pair(k)
        for y in range(Y):
            rows = pl.ds(pl.multiple_of((y * X + there) * (ZH * R), 32), ZH * R)
            share = jnp.dot(cot_t[rows, :], rounded, preferred_element_type=F32)
            acc[y, there] = share.reshape(ZH, R, C)
        copy.start()
    for k in range(Y):
        y_pair(k)[1].start()

    grad_output = scale_inv * (grad_normed - normed * jnp.mean(grad_normed * normed, axis=-1, keepdims=True))
    b_loc[:C, :] = mm(grad_output, query_scaled, TN)
    b_loc[C:, :] = jnp.broadcast_to(decay, (8, C))

    @pl.when(odd)
    def _():
        b_to_mate.start()

    x1 = Ring(
        xx, X, near_x, lambda dest, part: acc.at[4 * part : 4 * part + 4, dest, mine],
        ((0, 1, 2), (1, -1, 2), (1, 1, 1), (0, -1, 1)), x1_slots, x1_send, x1_recv,
    )
    y1 = Ring(
        yy, Y, near_y, lambda dest, part: acc.at[dest, 2 * part : 2 * part + 2, mine + 1],
        ((0, 1, 4), (1, -1, 4), (1, 1, 3), (0, -1, 3)), y1_slots, y1_send, y1_recv,
    )
    x2 = Ring(
        yy, Y, near_y, lambda dest, part: acc.at[dest, xx, mine],
        ((0, 1, 4), (0, -1, 3)), x2_slots, x2_send, x2_recv,
    )
    y2 = Ring(
        xx, X, near_x, lambda dest, part: acc.at[yy, dest, mine + 1],
        ((0, 1, 2), (0, -1, 1)), y2_slots, y2_send, y2_recv,
    )

    def take_x(k):
        there, copy = x_pair(k)
        copy.wait_recv()
        acc[:, there, mine] += pair_slots[0, :, there]

    def take_y(k):
        there, copy = y_pair(k)
        copy.wait_recv()
        acc[there, :, mine + 1] += pair_slots[1, there]

    take_x(0)
    x1.start(0)
    x1.start(1)
    take_x(1)
    x1.start(2)
    take_x(2)
    x1.start(3)
    take_x(3)
    take_y(0)
    y1.start(0)
    y1.start(1)
    take_y(1)
    y1.start(2)
    take_y(2)
    y1.start(3)
    for k in range(3, Y):
        take_y(k)

    @pl.when(even)
    def _():
        b_to_mate.wait_recv()
        b_pair[:C, :] = b_loc[C : C + 1, :] * b_mate[:C, :] + b_loc[:C, :]
        b_pair[C:, :] = b_loc[C:, :] * b_mate[C:, :]

        @pl.when(chip == 2)
        def _():
            for copy in b_first:
                copy.start()

        @pl.when(chip == 1)
        def _():
            for copy in b_middle:
                copy.start()

    y1.step(0, 1)
    y1.step(1, 1)
    x1.step(0, 1)
    x1.step(1, 1)
    y1.step(2, 1)
    y1.step(3, 1)
    pairs = mm(grad_output, value, NT) * lower
    grad_query = rising * (mm(pairs, key_scaled) + mm(grad_output, state_in))
    gq_ref[...] = grad_query.astype(BF16)
    y1.step(0, 2)
    y1.step(1, 2)
    y1.step(2, 2)
    y1.step(3, 2)
    for stream in range(4):
        x1.finish(stream)
    x2.start(0)
    x2.start(1)
    grad_key = falling * mm(pairs, query_scaled, TN)
    y1.step(0, 3)
    y1.step(1, 3)
    x2.step(0, 1)
    x2.step(1, 1)
    grad_value = mm(scores, grad_output, TN)
    for stream in range(4):
        y1.finish(stream)
    y2.start(0)
    y2.start(1)
    x2.step(0, 2)
    x2.step(1, 2)

    later_ref = w_out.at[0:C]
    carried(b_in, b_first, b_middle, 2, 0, later_ref)

    @pl.when(even)
    def _():
        later_ref[...] = b_mate[C : C + 1, :] * later_ref[...] + b_mate[:C, :]

    later = later_ref[...]
    y2.step(0, 1)
    x2.step(0, 3)
    grad_key += jnp.exp(total - cumul) * mm(value, later)
    gk_ref[...] = grad_key.astype(BF16)
    y2.finish(0)
    y2.finish(1)

    def z_copy(i):
        part = 0 if i < ZL else 1
        return pltpu.make_async_remote_copy(
            acc.at[yy, xx, mine + part],
            z_slots.at[zz],
            z_send.at[i],
            z_recv.at[zz],
            device_id=at(yy, xx, base_z + i, core),
            device_id_type=MESH,
        )

    def z_each(which, act):
        for i in which:

            @pl.when(base_z + i != zz)
            def _():
                act(z_copy(i))

    z_each(range(ZL, 2 * ZL), lambda copy: copy.start())
    x2.finish(0)
    x2.finish(1)
    z_each(range(ZL), lambda copy: copy.start())

    grad_value += mm(key_to_end, later, NT)
    gv_ref[...] = grad_value.astype(BF16)
    gate = query * grad_query - key * grad_key
    end_state = local + decay * state_in
    later_sum = jnp.sum(end_state * later, axis=0, keepdims=True)
    gd_ref[...] = mm(lower, gate, TN) + later_sum

    to_mate = pltpu.make_async_remote_copy(
        w_out.at[C : C + R], w_out.at[C + R :], w_send, w_recv, device_id=mate, device_id_type=MESH
    )

    @pl.when(gathers)
    def _():
        z_slots[zz] = acc[yy, xx, zz // ZL]
        for i in range(Z):

            @pl.when(zz != i)
            def _():
                pltpu.make_async_remote_copy(
                    z_slots.at[i], z_slots.at[i], z_send.at[0], z_recv.at[i], device_id=mate, device_id_type=MESH
                ).wait_recv()

        summed = z_slots[0]
        for i in range(1, Z):
            summed += z_slots[i]
        w_out[C : C + R, :] = summed
        to_mate.start()
        gw_ref[...] = summed
        to_mate.wait_send()

    @pl.when(jnp.logical_not(gathers))
    def _():
        to_mate.wait_recv()
        gw_ref[...] = w_out[C + R :, :]

    z_each(range(2 * ZL), lambda copy: copy.wait_send())
    for k in range(X):
        x_pair(k)[1].wait_send()
    for k in range(Y):
        y_pair(k)[1].wait_send()
    for ring in (x1, y1, x2, y2):
        ring.drain()

    @pl.when(even)
    def _():
        f_to_mate.wait_send()

        @pl.when(chip == 2)
        def _():
            for copy in b_first:
                copy.wait_send()

        @pl.when(chip == 1)
        def _():
            for copy in b_middle:
                copy.wait_send()

    @pl.when(odd)
    def _():
        b_to_mate.wait_send()

        @pl.when(chip == 0)
        def _():
            for copy in f_first:
                copy.wait_send()

        @pl.when(chip == 1)
        def _():
            for copy in f_middle:
                copy.wait_send()


def body(queries, key_vectors, value_vectors, log_decay, out_weight, cotangent):
    vmem, dma = pltpu.VMEM, pltpu.SemaphoreType.DMA

    def slots(count, *block):
        return [vmem((count, *block, R, C), F32), dma((count,)), dma((count,))]

    carried = [vmem((C + 8, C), F32)] * 3 + [vmem((2, C + 8, C), F32), dma, dma, dma((4,)), dma((2,))]
    outs = pl.pallas_call(
        kernel,
        out_shape=[jax.ShapeDtypeStruct((T, C), BF16)] * 3
        + [jax.ShapeDtypeStruct((T, C), F32), jax.ShapeDtypeStruct((R, C), F32)],
        in_specs=[pl.BlockSpec(memory_space=pl.ANY)] * 6,
        out_specs=[pl.BlockSpec(memory_space=pltpu.VMEM)] * 5,
        scratch_shapes=[vmem((T, C), BF16)] * 3
        + [vmem((T, C), F32), vmem((D, C), BF16), vmem((T, D), BF16), vmem((D, T), BF16), dma((6,))]
        + [vmem((Y, X, ZH, R, C), F32), vmem((2, Y, X, R, C), F32), dma((X + Y,)), dma((X + Y,))]
        + slots(6, 4) + slots(14, 2) + slots(7) + slots(3)
        + [vmem((Z, R, C), F32), dma((6,)), dma((Z,)), vmem((C + 2 * R, C), F32), dma, dma]
        + carried + carried,
        compiler_params=pltpu.CompilerParams(
            collective_id=0, has_side_effects=True, vmem_limit_bytes=60 * 1024 * 1024
        ),
    )(queries[0], key_vectors[0], value_vectors[0], log_decay[0], out_weight, cotangent[0])
    return tuple(out[None] for out in outs[:4]) + (outs[4],)


def solution(mesh):
    rows = P("dp", "ctx", None)
    return jax.shard_map(
        body,
        mesh=mesh,
        in_specs=(rows, rows, rows, rows, P(), rows),
        out_specs=(rows, rows, rows, rows, P("dp", None)),
        check_vma=False,
    )
```

time: 1630 us -> 66.2 us (0.04)
  waiting for transfers between devices: 1460 us -> 0 us
  blocking collectives: 99.5 us -> 0 us
  Pallas kernels: 0 us -> 58.2 us
  starting transfers between devices: 39.3 us -> 0 us
    unnamed x2 -> x0, waiting for transfers between devices: 1430 us -> none
    psum x1 -> x0, blocking collectives: 99.5 us -> none  [body(): grad_weight = lax.psum(row_share, 'ctx')]
    pallas_call x0 -> x1, Pallas kernels: none -> 58.2 us  [body(): pl.pallas_call(kernel, out_shape=[jax.ShapeDtypeStruct((T, C), BF16)] * 3...]
    ppermute x15 -> x0, starting transfers between devices: 39.3 us -> none  [shifted(): lax.ppermute(value, axis, [(source, source + steps) for source in range(l...]
    ppermute x15 -> x0, waiting for transfers between devices: 28.1 us -> none  [shifted(): lax.ppermute(value, axis, [(source, source + steps) for source in range(l...]
  transfers between devices with their start and end apart: 16 -> 0, of which waited for: 11 -> 0; matrix products, arithmetic and copies ran while one was open for 0% -> 0% of each run, Pallas kernels for 0% -> 0%
where the time goes in v1:
time: 66.2 us; the launch traced here: 65.8 us
  Pallas kernels  58.2 us (88%)
  local copies, waits for them, and re-layouts  6.93 us (10%)
    pallas_call x1, Pallas kernels, body(): pl.pallas_call(kernel, out_shape=[jax.ShapeDtypeStruct((T, C), BF16)] * 3...  58.2 us
    unnamed x5, local copies, waits for them, and re-layouts  6.93 us

profile of v1, /device:TPU:1, one launch (start us, length us, event | category | flops | bytes accessed | tf_op | source)
XLA Modules:
  0.0 65.8 jit_solution(16112140242686988607)
XLA Ops:
  0.6 58.2 %shard_map.101 = (bf16[128,128]{1,0:T(8,128)(2,1)}, bf16[128,128]{1,0:T(8,128)(2,1)}, bf16[128,128]{1,0:T(8,128)(2,1)}, f32[128,128]{1,0:T(8,128)}, f32[40,128]{1,0:T(8,128)}) custom-call(bf16[128,128]{1,0:T(8,128)(2,1)} %bitcast.12, bf16[128,128]{1,0:T(8,128)(2,1)} %bitcast.13, bf16[128,128]{1,0:T(8,128)(2,1)} %bitcast.14, f32[128,128]{1,0:T(8,128)} %bitcast.10, ...), custom_call_target="tpu_custom_call" | custom-call | tf_op jit(solution)/shard_map/pallas_call | solution.py:493
  58.8 1.4 %copy.16 = bf16[1,128,128]{2,1,0:T(8,128)(2,1)} copy(bf16[1,128,128]{2,1,0:T(8,128)(2,1)} %bitcast.17) | data formatting | bytes 65536
  60.2 1.4 %copy.17 = bf16[1,128,128]{2,1,0:T(8,128)(2,1)} copy(bf16[1,128,128]{2,1,0:T(8,128)(2,1)} %bitcast.16) | data formatting | bytes 65536
  61.6 1.4 %copy.18 = bf16[1,128,128]{2,1,0:T(8,128)(2,1)} copy(bf16[1,128,128]{2,1,0:T(8,128)(2,1)} %bitcast.15) | data formatting | bytes 65536
  63.0 1.5 %copy.19 = f32[1,128,128]{2,1,0:T(8,128)} copy(f32[1,128,128]{2,1,0:T(8,128)} %bitcast.11) | data formatting | bytes 131072
  64.4 1.3 %copy.20 = f32[40,128]{1,0:T(8,128)} copy(f32[40,128]{1,0:T(8,128)} %get-tuple-element.24) | data formatting | bytes 40960

commit v2 on v1

--- a/solution.py
+++ b/solution.py
@@ -14,6 +14,7 @@
 MESH = pl.DeviceIdType.MESH
 F32 = jnp.float32
 BF16 = jnp.bfloat16
+RESULTS = [((T, C), BF16)] * 3 + [((T, C), F32), ((R, C), F32)]
 
 
 def mm(a, b, dims=((1,), (0,)), precision=lax.Precision.HIGHEST):
@@ -67,6 +68,38 @@
         for index, (_, _, hops, _) in enumerate(self.streams):
             for turn in range(hops):
                 self.copy(index, turn).wait_send()
+
+
+class Direct:
+    def __init__(self, me, count, device, own, order, slots, send, recv):
+        self.me, self.count, self.device, self.own, self.order = me, count, device, own, order
+        self.slots, self.send, self.recv = slots, send, recv
+
+    def copy(self, index):
+        step = self.order[index]
+        return pltpu.make_async_remote_copy(
+            src_ref=self.own(lax.rem(self.me + step, self.count)),
+            dst_ref=self.slots.at[index],
+            send_sem=self.send.at[index],
+            recv_sem=self.recv.at[index],
+            device_id=self.device(step),
+            device_id_type=MESH,
+        )
+
+    def start(self):
+        for index in range(len(self.order)):
+            self.copy(index).start()
+
+    def finish(self):
+        total = self.own(self.me)[...]
+        for index in reversed(range(len(self.order))):
+            self.copy(index).wait_recv()
+            total += self.slots[index]
+        self.own(self.me)[...] = total
+
+    def drain(self):
+        for index in range(len(self.order)):
+            self.copy(index).wait_send()
 
 
 def kernel(
@@ -122,9 +155,10 @@
         for i in range(6):
             greet(at(yy, xx, base_z + i, core))
 
-    for sign in (1, -1):
-        greet(near_y(sign))
-        greet(near_x(sign))
+    for step in (4, 3, 5, 2, 6, 1, 7):
+        greet(near_y(step))
+    for step in (2, 1, 3):
+        greet(near_x(step))
     for step in range(1, 6):
         greet({"dp": dp, "ctx": lax.rem(ctx + step, 6)})
 
@@ -146,11 +180,11 @@
 
     @pl.when(gathers)
     def _():
-        pl.semaphore_wait(barrier, 20)
+        pl.semaphore_wait(barrier, 26)
 
     @pl.when(jnp.logical_not(gathers))
     def _():
-        pl.semaphore_wait(barrier, 15)
+        pl.semaphore_wait(barrier, 21)
 
     def far_sends(pair, slots, send, recv, first, last):
         def copy(slot, target, h, index):
@@ -270,9 +304,11 @@
             rows = pl.ds(pl.multiple_of((y * X + there) * (ZH * R), 32), ZH * R)
             share = jnp.dot(cot_t[rows, :], rounded, preferred_element_type=F32)
             acc[y, there] = share.reshape(ZH, R, C)
-        copy.start()
-    for k in range(Y):
-        y_pair(k)[1].start()
+        if k == 0:
+            copy.start()
+    halves = (("y", 0), ("x", 1), ("y", 1), ("y", 2), ("x", 2), ("x", 3)) + tuple(("y", k) for k in range(3, Y))
+    for axis, k in halves:
+        (x_pair if axis == "x" else y_pair)(k)[1].start()
 
     grad_output = scale_inv * (grad_normed - normed * jnp.mean(grad_normed * normed, axis=-1, keepdims=True))
     b_loc[:C, :] = mm(grad_output, query_scaled, TN)
@@ -290,14 +326,8 @@
         yy, Y, near_y, lambda dest, part: acc.at[dest, 2 * part : 2 * part + 2, mine + 1],
         ((0, 1, 4), (1, -1, 4), (1, 1, 3), (0, -1, 3)), y1_slots, y1_send, y1_recv,
     )
-    x2 = Ring(
-        yy, Y, near_y, lambda dest, part: acc.at[dest, xx, mine],
-        ((0, 1, 4), (0, -1, 3)), x2_slots, x2_send, x2_recv,
-    )
-    y2 = Ring(
-        xx, X, near_x, lambda dest, part: acc.at[yy, dest, mine + 1],
-        ((0, 1, 2), (0, -1, 1)), y2_slots, y2_send, y2_recv,
-    )
+    x2 = Direct(yy, Y, near_y, lambda dest: acc.at[dest, xx, mine], (4, 3, 5, 2, 6, 1, 7), x2_slots, x2_send, x2_recv)
+    y2 = Direct(xx, X, near_x, lambda dest: acc.at[yy, dest, mine + 1], (2, 1, 3), y2_slots, y2_send, y2_recv)
 
     def take_x(k):
         there, copy = x_pair(k)
@@ -312,18 +342,18 @@
     take_x(0)
     x1.start(0)
     x1.start(1)
-    take_x(1)
-    x1.start(2)
-    take_x(2)
-    x1.start(3)
-    take_x(3)
     take_y(0)
     y1.start(0)
     y1.start(1)
+    take_x(1)
+    x1.start(2)
     take_y(1)
     y1.start(2)
     take_y(2)
     y1.start(3)
+    take_x(2)
+    x1.start(3)
+    take_x(3)
     for k in range(3, Y):
         take_y(k)
 
@@ -350,28 +380,22 @@
     y1.step(2, 1)
     y1.step(3, 1)
     pairs = mm(grad_output, value, NT) * lower
+    y1.step(0, 2)
+    y1.step(1, 2)
     grad_query = rising * (mm(pairs, key_scaled) + mm(grad_output, state_in))
     gq_ref[...] = grad_query.astype(BF16)
-    y1.step(0, 2)
-    y1.step(1, 2)
     y1.step(2, 2)
     y1.step(3, 2)
-    for stream in range(4):
+    for stream in (2, 3, 0, 1):
         x1.finish(stream)
-    x2.start(0)
-    x2.start(1)
-    grad_key = falling * mm(pairs, query_scaled, TN)
+    x2.start()
     y1.step(0, 3)
     y1.step(1, 3)
-    x2.step(0, 1)
-    x2.step(1, 1)
+    grad_key = falling * mm(pairs, query_scaled, TN)
+    for stream in (2, 3, 0, 1):
+        y1.finish(stream)
+    y2.start()
     grad_value = mm(scores, grad_output, TN)
-    for stream in range(4):
-        y1.finish(stream)
-    y2.start(0)
-    y2.start(1)
-    x2.step(0, 2)
-    x2.step(1, 2)
 
     later_ref = w_out.at[0:C]
     carried(b_in, b_first, b_middle, 2, 0, later_ref)
@@ -381,12 +405,9 @@
         later_ref[...] = b_mate[C : C + 1, :] * later_ref[...] + b_mate[:C, :]
 
     later = later_ref[...]
-    y2.step(0, 1)
-    x2.step(0, 3)
     grad_key += jnp.exp(total - cumul) * mm(value, later)
     gk_ref[...] = grad_key.astype(BF16)
-    y2.finish(0)
-    y2.finish(1)
+    x2.finish()
 
     def z_copy(i):
         part = 0 if i < ZL else 1
@@ -406,10 +427,9 @@
             def _():
                 act(z_copy(i))
 
+    z_each(range(ZL), lambda copy: copy.start())
+    y2.finish()
     z_each(range(ZL, 2 * ZL), lambda copy: copy.start())
-    x2.finish(0)
-    x2.finish(1)
-    z_each(range(ZL), lambda copy: copy.start())
 
     grad_value += mm(key_to_end, later, NT)
     gv_ref[...] = grad_value.astype(BF16)
@@ -483,6 +503,14 @@
                 copy.wait_send()
 
 
+def store(*refs):
+    copies = [pltpu.make_async_copy(refs[i], refs[5 + i], refs[10].at[i]) for i in range(5)]
+    for copy in copies:
+        copy.start()
+    for copy in copies:
+        copy.wait()
+
+
 def body(queries, key_vectors, value_vectors, log_decay, out_weight, cotangent):
     vmem, dma = pltpu.VMEM, pltpu.SemaphoreType.DMA
 
@@ -492,9 +520,8 @@
     carried = [vmem((C + 8, C), F32)] * 3 + [vmem((2, C + 8, C), F32), dma, dma, dma((4,)), dma((2,))]
     outs = pl.pallas_call(
         kernel,
-        out_shape=[jax.ShapeDtypeStruct((T, C), BF16)] * 3
-        + [jax.ShapeDtypeStruct((T, C), F32), jax.ShapeDtypeStruct((R, C), F32)],
-        in_specs=[pl.BlockSpec(memory_space=pl.ANY)] * 6,
+        out_shape=[pltpu.VMEM(shape, dtype) for shape, dtype in RESULTS],
+        in_specs=[pl.BlockSpec(memory_space=pltpu.HBM)] * 6,
         out_specs=[pl.BlockSpec(memory_space=pltpu.VMEM)] * 5,
         scratch_shapes=[vmem((T, C), BF16)] * 3
         + [vmem((T, C), F32), vmem((D, C), BF16), vmem((T, D), BF16), vmem((D, T), BF16), dma((6,))]
@@ -506,6 +533,14 @@
             collective_id=0, has_side_effects=True, vmem_limit_bytes=60 * 1024 * 1024
         ),
     )(queries[0], key_vectors[0], value_vectors[0], log_decay[0], out_weight, cotangent[0])
+    outs = pl.pallas_call(
+        store,
+        out_shape=[jax.ShapeDtypeStruct(shape, dtype) for shape, dtype in RESULTS],
+        in_specs=[pl.BlockSpec(memory_space=pl.ANY)] * 5,
+        out_specs=[pl.BlockSpec(memory_space=pl.ANY)] * 5,
+        scratch_shapes=[dma((5,))],
+        compiler_params=pltpu.CompilerParams(vmem_limit_bytes=1024 * 1024),
+    )(*outs)
     return tuple(out[None] for out in outs[:4]) + (outs[4],)
 
 

time: 66.2 us -> 52.5 us (0.79)
  local copies, waits for them, and re-layouts: 6.93 us -> 0 us
  Pallas kernels: 58.2 us -> 51.7 us
    unnamed x5 -> x0, local copies, waits for them, and re-layouts: 6.93 us -> none
    pallas_call x1 -> x2, Pallas kernels: 58.2 us -> 51.7 us  [the longest x1 51 us: body(): pl.pallas_call(kernel, out_shape=[pltpu.VMEM(shape, dtype) for shape, dty...]
where the time goes in v2:
time: 52.5 us; the launch traced here: 52.3 us
  Pallas kernels  51.7 us (98%)
  between operations  0.64 us (1%)
    pallas_call x1, Pallas kernels, body(): pl.pallas_call(kernel, out_shape=[pltpu.VMEM(shape, dtype) for shape, dty...  51 us

profile of v2, /device:TPU:1, one launch (start us, length us, event | category | flops | bytes accessed | tf_op | source)
XLA Modules:
  0.0 52.3 jit_solution(18196533956345620478)
XLA Ops:
  0.6 51.0 %shard_map.101 = (bf16[128,128]{1,0:T(8,128)(2,1)S(1)}, bf16[128,128]{1,0:T(8,128)(2,1)S(1)}, bf16[128,128]{1,0:T(8,128)(2,1)S(1)}, f32[128,128]{1,0:T(8,128)S(1)}, f32[40,128]{1,0:T(8,128)S(1)}) custom-call(bf16[128,128]{1,0:T(8,128)(2,1)} %bitcast.11, bf16[128,128]{1,0:T(8,128)(2,1)} %bitcast.12, bf16[128,128]{1,0:T(8,128)(2,1)} %bitcast.13, ...), custom_call_target="tpu_custom_call" | custom-call | tf_op jit(solution)/shard_map/pallas_call | solution.py:521
  51.6 0.7 %shard_map.102 = (bf16[128,128]{1,0:T(8,128)(2,1)}, bf16[128,128]{1,0:T(8,128)(2,1)}, bf16[128,128]{1,0:T(8,128)(2,1)}, f32[128,128]{1,0:T(8,128)}, f32[40,128]{1,0:T(8,128)}) custom-call(bf16[128,128]{1,0:T(8,128)(2,1)S(1)} %get-tuple-element.15.refs_0_, bf16[128,128]{1,0:T(8,128)(2,1)S(1)} %get-tuple-element.16.refs_1_, ...), custom_call_target="tpu_custom_call" | custom-call | tf_op jit(solution)/shard_map/pallas_call | solution.py:536

commit v3 on v2

--- a/solution.py
+++ b/solution.py
@@ -107,11 +107,11 @@
     gq_ref, gk_ref, gv_ref, gd_ref, gw_ref,
     q_in, k_in, v_in, decay_in, weight_in, cot_in, cot_t, in_sem,
     acc, pair_slots, pair_send, pair_recv,
-    x1_slots, x1_send, x1_recv, y1_slots, y1_send, y1_recv,
+    x1_slots, x1_send, x1_recv, y1_slots, y1_send, y1_recv, far_slots, far_send, far_recv,
     x2_slots, x2_send, x2_recv, y2_slots, y2_send, y2_recv,
     z_slots, z_send, z_recv, w_out, w_send, w_recv,
     f_loc, f_mate, f_pair, f_in, f_mate_send, f_mate_recv, f_send, f_recv,
-    b_loc, b_mate, b_pair, b_in, b_mate_send, b_mate_recv, b_send, b_recv,
+    b_loc, b_mate, b_pair, b_in, b_mate_send, b_mate_recv, b_send, b_recv, y_here, z_here,
 ):
     dp, ctx = lax.axis_index("dp"), lax.axis_index("ctx")
     yy = dp // (X * ZH)
@@ -145,17 +145,9 @@
     def greet(device):
         pl.semaphore_signal(barrier, inc=1, device_id=device, device_id_type=MESH)
 
-    @pl.when(gathers)
-    def _():
-        for far in (6, 5, 7, 4, 8, 3, 9, 2, 10, 1, 11):
-            greet(at(yy, xx, lax.rem(zz + far, Z), core))
-
-    @pl.when(jnp.logical_not(gathers))
-    def _():
-        for i in range(6):
-            greet(at(yy, xx, base_z + i, core))
-
-    for step in (4, 3, 5, 2, 6, 1, 7):
+    for step in (3, 9, 2, 10, 1, 11):
+        greet(at(yy, xx, lax.rem(zz + step, Z), core))
+    for step in (2, 6, 1, 7):
         greet(near_y(step))
     for step in (2, 1, 3):
         greet(near_x(step))
@@ -178,13 +170,10 @@
     f_loc[:C, :] = local
     f_loc[C:, :] = jnp.broadcast_to(decay, (8, C))
 
-    @pl.when(gathers)
-    def _():
-        pl.semaphore_wait(barrier, 26)
-
-    @pl.when(jnp.logical_not(gathers))
-    def _():
-        pl.semaphore_wait(barrier, 21)
+    pl.semaphore_wait(barrier, 18)
+
+    def relay(sem, device):
+        pl.semaphore_signal(sem, inc=1, device_id=device, device_id_type=MESH)
 
     def far_sends(pair, slots, send, recv, first, last):
         def copy(slot, target, h, index):
@@ -211,6 +200,11 @@
     @pl.when(even)
     def _():
         f_to_mate.start()
+
+    for step in (3, 9):
+        relay(z_here, at(yy, xx, lax.rem(zz + step, Z), core))
+    for step in (2, 6):
+        relay(y_here, near_y(step))
 
     loads[3].wait()
     query = q_in[...].astype(F32)
@@ -274,7 +268,7 @@
 
     mine, theirs = 2 * core, 2 * (1 - core)
     x_order = (2, 1, 3, 0)
-    y_order = (4, 3, 5, 2, 6, 1, 7, 0)
+    y_order = (3, 5, 4, 2, 6, 1, 7, 0)
 
     def x_pair(k):
         there = lax.rem(xx + x_order[k], X)
@@ -298,15 +292,15 @@
             device_id_type=MESH,
         )
 
-    for k in range(X):
-        there, copy = x_pair(k)
-        for y in range(Y):
-            rows = pl.ds(pl.multiple_of((y * X + there) * (ZH * R), 32), ZH * R)
+    for k in range(Y):
+        there, copy = y_pair(k)
+        for x in range(X):
+            rows = pl.ds(pl.multiple_of((there * X + x) * (ZH * R), 32), ZH * R)
             share = jnp.dot(cot_t[rows, :], rounded, preferred_element_type=F32)
-            acc[y, there] = share.reshape(ZH, R, C)
-        if k == 0:
+            acc[there, x] = share.reshape(ZH, R, C)
+        if k < 3:
             copy.start()
-    halves = (("y", 0), ("x", 1), ("y", 1), ("y", 2), ("x", 2), ("x", 3)) + tuple(("y", k) for k in range(3, Y))
+    halves = (("x", 0), ("x", 1), ("x", 2), ("y", 3), ("y", 4), ("x", 3)) + tuple(("y", k) for k in range(5, Y))
     for axis, k in halves:
         (x_pair if axis == "x" else y_pair)(k)[1].start()
 
@@ -324,8 +318,9 @@
     )
     y1 = Ring(
         yy, Y, near_y, lambda dest, part: acc.at[dest, 2 * part : 2 * part + 2, mine + 1],
-        ((0, 1, 4), (1, -1, 4), (1, 1, 3), (0, -1, 3)), y1_slots, y1_send, y1_recv,
-    )
+        ((0, 1, 3), (0, -1, 3), (1, 1, 3), (1, -1, 3)), y1_slots, y1_send, y1_recv,
+    )
+    far_y = Direct(yy, Y, near_y, lambda dest: acc.at[dest, :, mine + 1], (4,), far_slots, far_send, far_recv)
     x2 = Direct(yy, Y, near_y, lambda dest: acc.at[dest, xx, mine], (4, 3, 5, 2, 6, 1, 7), x2_slots, x2_send, x2_recv)
     y2 = Direct(xx, X, near_x, lambda dest: acc.at[yy, dest, mine + 1], (2, 1, 3), y2_slots, y2_send, y2_recv)
 
@@ -339,20 +334,22 @@
         copy.wait_recv()
         acc[there, :, mine + 1] += pair_slots[1, there]
 
+    take_y(0)
+    y1.start(0)
+    y1.start(2)
+    take_y(1)
+    y1.start(1)
+    y1.start(3)
     take_x(0)
     x1.start(0)
     x1.start(1)
-    take_y(0)
-    y1.start(0)
-    y1.start(1)
     take_x(1)
     x1.start(2)
-    take_y(1)
-    y1.start(2)
-    take_y(2)
-    y1.start(3)
     take_x(2)
     x1.start(3)
+    take_y(2)
+    pl.semaphore_wait(y_here, 2)
+    far_y.start()
     take_x(3)
     for k in range(3, Y):
         take_y(k)
@@ -389,11 +386,10 @@
     for stream in (2, 3, 0, 1):
         x1.finish(stream)
     x2.start()
-    y1.step(0, 3)
-    y1.step(1, 3)
     grad_key = falling * mm(pairs, query_scaled, TN)
     for stream in (2, 3, 0, 1):
         y1.finish(stream)
+    far_y.finish()
     y2.start()
     grad_value = mm(scores, grad_output, TN)
 
@@ -427,6 +423,7 @@
             def _():
                 act(z_copy(i))
 
+    pl.semaphore_wait(z_here, 2)
     z_each(range(ZL), lambda copy: copy.start())
     y2.finish()
     z_each(range(ZL, 2 * ZL), lambda copy: copy.start())
@@ -471,7 +468,7 @@
         x_pair(k)[1].wait_send()
     for k in range(Y):
         y_pair(k)[1].wait_send()
-    for ring in (x1, y1, x2, y2):
+    for ring in (x1, y1, far_y, x2, y2):
         ring.drain()
 
     @pl.when(even)
@@ -526,9 +523,9 @@
         scratch_shapes=[vmem((T, C), BF16)] * 3
         + [vmem((T, C), F32), vmem((D, C), BF16), vmem((T, D), BF16), vmem((D, T), BF16), dma((6,))]
         + [vmem((Y, X, ZH, R, C), F32), vmem((2, Y, X, R, C), F32), dma((X + Y,)), dma((X + Y,))]
-        + slots(6, 4) + slots(14, 2) + slots(7) + slots(3)
+        + slots(6, 4) + slots(12, 2) + slots(1, X) + slots(7) + slots(3)
         + [vmem((Z, R, C), F32), dma((6,)), dma((Z,)), vmem((C + 2 * R, C), F32), dma, dma]
-        + carried + carried,
+        + carried + carried + [pltpu.SemaphoreType.REGULAR] * 2,
         compiler_params=pltpu.CompilerParams(
             collective_id=0, has_side_effects=True, vmem_limit_bytes=60 * 1024 * 1024
         ),

time: 52.5 us -> 51.1 us (0.973)
  Pallas kernels: 51.7 us -> 50.3 us
    pallas_call x1, Pallas kernels: 51 us -> 49.6 us  [body(): pl.pallas_call(kernel, out_shape=[pltpu.VMEM(shape, dtype) for shape, dty...]
where the time goes in v3:
time: 51.1 us; the launch traced here: 50.9 us
  Pallas kernels  50.3 us (98%)
  between operations  0.64 us (1%)
    pallas_call x1, Pallas kernels, body(): pl.pallas_call(kernel, out_shape=[pltpu.VMEM(shape, dtype) for shape, dty...  49.6 us

profile of v3, /device:TPU:1, one launch (start us, length us, event | category | flops | bytes accessed | tf_op | source)
XLA Modules:
  0.0 50.9 jit_solution(13445640381541930371)
XLA Ops:
  0.6 49.6 %shard_map.101 = (bf16[128,128]{1,0:T(8,128)(2,1)S(1)}, bf16[128,128]{1,0:T(8,128)(2,1)S(1)}, bf16[128,128]{1,0:T(8,128)(2,1)S(1)}, f32[128,128]{1,0:T(8,128)S(1)}, f32[40,128]{1,0:T(8,128)S(1)}) custom-call(bf16[128,128]{1,0:T(8,128)(2,1)} %bitcast.11, bf16[128,128]{1,0:T(8,128)(2,1)} %bitcast.12, bf16[128,128]{1,0:T(8,128)(2,1)} %bitcast.13, ...), custom_call_target="tpu_custom_call" | custom-call | tf_op jit(solution)/shard_map/pallas_call | solution.py:518
  50.2 0.7 %shard_map.102 = (bf16[128,128]{1,0:T(8,128)(2,1)}, bf16[128,128]{1,0:T(8,128)(2,1)}, bf16[128,128]{1,0:T(8,128)(2,1)}, f32[128,128]{1,0:T(8,128)}, f32[40,128]{1,0:T(8,128)}) custom-call(bf16[128,128]{1,0:T(8,128)(2,1)S(1)} %get-tuple-element.15.refs_0_, bf16[128,128]{1,0:T(8,128)(2,1)S(1)} %get-tuple-element.16.refs_1_, ...), custom_call_target="tpu_custom_call" | custom-call | tf_op jit(solution)/shard_map/pallas_call | solution.py:533

commit v4 on v3

--- a/solution.py
+++ b/solution.py
@@ -186,7 +186,13 @@
         from_middle = [copy(1, last, h, h) for h in (0, 1)]
         return from_first, from_middle
 
-    f_first, f_middle = far_sends(f_pair, f_in, f_send, f_recv, 0, 2)
+    def f_onward(slot, target, index):
+        return pltpu.make_async_remote_copy(
+            f_pair, f_in.at[slot], f_send.at[index], f_recv.at[slot],
+            device_id={"dp": dp, "ctx": 2 * target + core}, device_id_type=MESH,
+        )
+
+    f_first, f_middle = [f_onward(0, 2, 0), f_onward(0, 1, 1)], [f_onward(1, 2, 0)]
     b_first, b_middle = far_sends(b_pair, b_in, b_send, b_recv, 2, 0)
     f_to_mate = pltpu.make_async_remote_copy(
         f_loc, f_mate, f_mate_send, f_mate_recv, device_id=mate, device_id_type=MESH
@@ -197,9 +203,7 @@
     even = core == 0
     odd = core == 1
 
-    @pl.when(even)
-    def _():
-        f_to_mate.start()
+    f_to_mate.start()
 
     for step in (3, 9):
         relay(z_here, at(yy, xx, lax.rem(zz + step, Z), core))
@@ -214,21 +218,27 @@
     key_scaled = key * falling
     scores = mm(query_scaled, key_scaled, NT) * lower
 
+    f_to_mate.wait_recv()
+
     @pl.when(odd)
     def _():
-        f_to_mate.wait_recv()
         f_pair[:C, :] = f_loc[C : C + 1, :] * f_mate[:C, :] + f_loc[:C, :]
-        f_pair[C:, :] = f_loc[C:, :] * f_mate[C:, :]
-
-        @pl.when(chip == 0)
-        def _():
-            for copy in f_first:
-                copy.start()
-
-        @pl.when(chip == 1)
-        def _():
-            for copy in f_middle:
-                copy.start()
+
+    @pl.when(even)
+    def _():
+        f_pair[:C, :] = f_mate[C : C + 1, :] * f_loc[:C, :] + f_mate[:C, :]
+
+    f_pair[C:, :] = f_loc[C:, :] * f_mate[C:, :]
+
+    @pl.when(chip == 0)
+    def _():
+        for copy in f_first:
+            copy.start()
+
+    @pl.when(chip == 1)
+    def _():
+        for copy in f_middle:
+            copy.start()
 
     within = mm(scores, value)
     loads[4].wait()
@@ -473,8 +483,6 @@
 
     @pl.when(even)
     def _():
-        f_to_mate.wait_send()
-
         @pl.when(chip == 2)
         def _():
             for copy in b_first:
@@ -489,15 +497,17 @@
     def _():
         b_to_mate.wait_send()
 
-        @pl.when(chip == 0)
-        def _():
-            for copy in f_first:
-                copy.wait_send()
-
-        @pl.when(chip == 1)
-        def _():
-            for copy in f_middle:
-                copy.wait_send()
+    f_to_mate.wait_send()
+
+    @pl.when(chip == 0)
+    def _():
+        for copy in f_first:
+            copy.wait_send()
+
+    @pl.when(chip == 1)
+    def _():
+        for copy in f_middle:
+            copy.wait_send()
 
 
 def store(*refs):

time: 51.1 us -> 52 us (1.018)
  Pallas kernels: 50.3 us -> 51.3 us
    pallas_call x1, Pallas kernels: 49.6 us -> 50.5 us  [body(): pl.pallas_call(kernel, out_shape=[pltpu.VMEM(shape, dtype) for shape, dty...]
where the time goes in v4:
time: 52 us; the launch traced here: 51.9 us
  Pallas kernels  51.3 us (99%)
  between operations  0.64 us (1%)
    pallas_call x1, Pallas kernels, body(): pl.pallas_call(kernel, out_shape=[pltpu.VMEM(shape, dtype) for shape, dty...  50.5 us

profile of v4, /device:TPU:1, one launch (start us, length us, event | category | flops | bytes accessed | tf_op | source)
XLA Modules:
  0.0 51.9 jit_solution(15004247928260600257)
XLA Ops:
  0.6 50.5 %shard_map.101 = (bf16[128,128]{1,0:T(8,128)(2,1)S(1)}, bf16[128,128]{1,0:T(8,128)(2,1)S(1)}, bf16[128,128]{1,0:T(8,128)(2,1)S(1)}, f32[128,128]{1,0:T(8,128)S(1)}, f32[40,128]{1,0:T(8,128)S(1)}) custom-call(bf16[128,128]{1,0:T(8,128)(2,1)} %bitcast.11, bf16[128,128]{1,0:T(8,128)(2,1)} %bitcast.12, bf16[128,128]{1,0:T(8,128)(2,1)} %bitcast.13, ...), custom_call_target="tpu_custom_call" | custom-call | tf_op jit(solution)/shard_map/pallas_call | solution.py:528
  51.2 0.7 %shard_map.102 = (bf16[128,128]{1,0:T(8,128)(2,1)}, bf16[128,128]{1,0:T(8,128)(2,1)}, bf16[128,128]{1,0:T(8,128)(2,1)}, f32[128,128]{1,0:T(8,128)}, f32[40,128]{1,0:T(8,128)}) custom-call(bf16[128,128]{1,0:T(8,128)(2,1)S(1)} %get-tuple-element.15.refs_0_, bf16[128,128]{1,0:T(8,128)(2,1)S(1)} %get-tuple-element.16.refs_1_, ...), custom_call_target="tpu_custom_call" | custom-call | tf_op jit(solution)/shard_map/pallas_call | solution.py:543
